TPU v7x, 32 devices: a whole 2x2x4 slice. The times are simulated.
32 devices in a mesh: seq: 4 (over y, x), fsdp: 8 (over z, core).
Axes of the slice: x: 2, y: 2, z: 4, core: 2. Of those that a mesh axis runs over, the one named last changes fastest.
Arguments:
- tokens: bfloat16 [8, 1024, 1024], P('fsdp', 'seq'), may hold values from -6 to 6
- segments: int32 [8, 1024], P('fsdp', 'seq'), may hold values from 0 to 2, as said below
- qkv_weight: bfloat16 [1024, 3072], P(('seq', 'fsdp')), may hold values from -0.1875 to 0.1875
- out_weight: bfloat16 [1024, 1024], P(('seq', 'fsdp')), may hold values from -0.1875 to 0.1875
- up_weight: bfloat16 [1024, 4096], P(('seq', 'fsdp')), may hold values from -0.1875 to 0.1875
- up_bias: bfloat16 [4096], P(('seq', 'fsdp')), may hold values from -3 to 3
- down_weight: bfloat16 [4096, 1024], P(('seq', 'fsdp')), may hold values from -0.09375 to 0.09375
- first_gain: bfloat16 [1024], P(('seq', 'fsdp')), may hold values from 0.5 to 1.5
- first_shift: bfloat16 [1024], P(('seq', 'fsdp')), may hold values from -3 to 3
- second_gain: bfloat16 [1024], P(('seq', 'fsdp')), may hold values from 0.5 to 1.5
- second_shift: bfloat16 [1024], P(('seq', 'fsdp')), may hold values from -3 to 3
- third_gain: bfloat16 [1024], P(('seq', 'fsdp')), may hold values from 0.5 to 1.5
- third_shift: bfloat16 [1024], P(('seq', 'fsdp')), may hold values from -3 to 3
- fourth_gain: bfloat16 [1024], P(('seq', 'fsdp')), may hold values from 0.5 to 1.5
- fourth_shift: bfloat16 [1024], P(('seq', 'fsdp')), may hold values from -3 to 3
- out_cotangent: bfloat16 [8, 1024, 1024], P('fsdp', 'seq'), may hold values from -6 to 6
Outputs:
- layer_out: bfloat16 [8, 1024, 1024], P('fsdp', 'seq')
- tokens_grad: float32 [8, 1024, 1024], P('fsdp', 'seq')
- qkv_weight_grad: float32 [1024, 3072], P(('seq', 'fsdp'))
- out_weight_grad: float32 [1024, 1024], P(('seq', 'fsdp'))
- up_weight_grad: float32 [1024, 4096], P(('seq', 'fsdp'))
- up_bias_grad: float32 [4096], P(('seq', 'fsdp'))
- down_weight_grad: float32 [4096, 1024], P(('seq', 'fsdp'))
- first_gain_grad: float32 [1024], P(('seq', 'fsdp'))
- first_shift_grad: float32 [1024], P(('seq', 'fsdp'))
- second_gain_grad: float32 [1024], P(('seq', 'fsdp'))
- second_shift_grad: float32 [1024], P(('seq', 'fsdp'))
- third_gain_grad: float32 [1024], P(('seq', 'fsdp'))
- third_shift_grad: float32 [1024], P(('seq', 'fsdp'))
- fourth_gain_grad: float32 [1024], P(('seq', 'fsdp'))
- fourth_shift_grad: float32 [1024], P(('seq', 'fsdp'))
Inputs may be any that keep to these rules, and one draw needn't show every extreme that they name: `segments`: within a sequence document numbers never fall; each sequence holds 3 documents of 200 to 512 tokens, one of exactly 512.
All inputs are finite; a program needn't handle non-finite values.
Results may differ from a plain program's by a relative error of at most 0.012.
Values may be sent and summed in bfloat16 or wider, within the bound.
A program may use at most 192 MiB of HBM per device.

v0:
```python
from functools import partial
import jax
import jax.numpy as jnp
from jax import lax
from jax.sharding import PartitionSpec as P

HEAD_DIM = 64
F32 = jnp.float32
BF16 = jnp.bfloat16


def layer_norm(value, gain, shift):
    center = value - jnp.mean(value, -1, keepdims=True)
    spread = jnp.mean(center * center, -1, keepdims=True)
    return center * lax.rsqrt(spread + 1e-05) * gain + shift


def norm_pull(value, gain, grad):
    center = value - jnp.mean(value, -1, keepdims=True)
    spread = jnp.mean(center * center, -1, keepdims=True)
    scale = lax.rsqrt(spread + 1e-05)
    unit = center * scale
    pulled = grad * gain
    first = jnp.mean(pulled, -1, keepdims=True)
    second = jnp.mean(pulled * unit, -1, keepdims=True)
    return (scale * (pulled - first - unit * second), jnp.sum(grad * unit, 0), jnp.sum(grad, 0))


def dot(left, right, dims):
    return lax.dot_general(left, right, (dims, ((), ())), preferred_element_type=F32)


def attention(triple, segment_all, grad_of):
    length = triple.shape[0]
    group = triple.shape[1] // (3 * HEAD_DIM)
    heads = triple.reshape(length, 3, group, HEAD_DIM)
    query, keys, values = (heads[:, 0], heads[:, 1], heads[:, 2])
    places = jnp.arange(length, dtype=jnp.int32)
    allowed = (segment_all[:, None] == segment_all[None, :]) & (places[None, :] <= places[:, None])
    scores = jnp.einsum("qhd,khd->hqk", query, keys, preferred_element_type=F32) * 0.125
    scores = jnp.where(allowed[None], scores, -jnp.inf)
    row_max = jnp.max(scores, -1, keepdims=True)
    expo = jnp.exp(scores - row_max)
    totals = jnp.sum(expo, -1, keepdims=True)
    probs = expo / totals
    probs_low = probs.astype(BF16)
    attended = jnp.einsum("hqk,khd->qhd", probs_low, values, preferred_element_type=F32)
    attended = attended.astype(BF16).reshape(length, -1)

    def pull(grad):
        grad = grad.reshape(length, group, HEAD_DIM)
        grad_probs = jnp.einsum("qhd,khd->hqk", grad, values, preferred_element_type=F32)
        inner_sum = jnp.sum(probs * grad_probs, -1, keepdims=True)
        grad_scores = (probs * (grad_probs - inner_sum)).astype(BF16)
        grad_query = (
            jnp.einsum("hqk,khd->qhd", grad_scores, keys, preferred_element_type=F32) * 0.125
        )
        grad_keys = (
            jnp.einsum("hqk,qhd->khd", grad_scores, query, preferred_element_type=F32) * 0.125
        )
        grad_values = jnp.einsum("hqk,qhd->khd", probs_low, grad, preferred_element_type=F32)
        stacked = jnp.stack([grad_query, grad_keys, grad_values], 1)
        return stacked.astype(BF16).reshape(length, -1)

    return (attended, pull)


def on_device(
    tokens,
    segments,
    qkv_weight,
    out_weight,
    up_weight,
    up_bias,
    down_weight,
    first_gain,
    first_shift,
    second_gain,
    second_shift,
    third_gain,
    third_shift,
    fourth_gain,
    fourth_shift,
    out_cotangent,
):
    n_seq = lax.axis_size("seq")
    n_fsdp = lax.axis_size("fsdp")
    width = tokens.shape[2]

    def columns(weight, parts):
        rows = weight.shape[0]
        cut = weight.reshape(rows, parts, n_seq, -1).transpose(2, 0, 1, 3).reshape(n_seq, rows, -1)
        cut = lax.all_to_all(cut, "seq", split_axis=0, concat_axis=0, tiled=True)
        whole = lax.all_gather(cut, "fsdp", axis=1, tiled=True)
        return whole.reshape(n_seq * n_fsdp * rows, -1)

    def columns_back(grad, parts):
        rows = grad.shape[0] // (n_seq * n_fsdp)
        cut = grad.astype(BF16).reshape(n_seq, n_fsdp, rows, -1).transpose(1, 0, 2, 3)
        cut = lax.psum_scatter(cut, "fsdp", scatter_dimension=0, tiled=True)[0]
        cut = lax.all_to_all(cut, "seq", split_axis=0, concat_axis=0, tiled=True)
        cut = cut.reshape(n_seq, rows, parts, -1).transpose(1, 2, 0, 3)
        return cut.reshape(rows, -1).astype(F32)

    def rows_back(grad):
        return lax.psum_scatter(grad.astype(BF16), "fsdp", scatter_dimension=0, tiled=True).astype(
            F32
        )

    def spread_rows(value):
        return lax.all_gather(value, "seq", axis=0, tiled=True)

    def sum_rows(value):
        return lax.psum_scatter(value.astype(BF16), "seq", scatter_dimension=0, tiled=True).astype(
            F32
        )

    segment_all = lax.all_gather(segments[0], "seq", axis=0, tiled=True)
    small = jnp.stack(
        [
            first_gain,
            first_shift,
            second_gain,
            second_shift,
            third_gain,
            third_shift,
            fourth_gain,
            fourth_shift,
        ]
    )
    small = lax.all_gather(small, ("seq", "fsdp"), axis=1, tiled=True).astype(F32)
    gain_a, shift_a, gain_b, shift_b, gain_c, shift_c, gain_d, shift_d = small
    qkv_w = columns(qkv_weight, 3)
    out_w = lax.all_gather(out_weight, "fsdp", axis=0, tiled=True)
    up_w = columns(up_weight, 1)
    up_b = lax.all_gather(up_bias, "fsdp", axis=0, tiled=True).astype(F32)
    down_w = lax.all_gather(down_weight, "fsdp", axis=0, tiled=True)
    inputs = tokens[0].astype(F32)
    cotangent = out_cotangent[0].astype(F32)
    normed = spread_rows(layer_norm(inputs, gain_a, shift_a).astype(BF16))
    triple = dot(normed, qkv_w, ((1,), (0,))).astype(BF16)
    attended, attend_pull = attention(triple, segment_all, None)
    branch = sum_rows(dot(attended, out_w, ((1,), (0,))))
    middle = inputs + layer_norm(branch, gain_b, shift_b)
    inner = spread_rows(layer_norm(middle, gain_c, shift_c).astype(BF16))
    pre = dot(inner, up_w, ((1,), (0,))) + up_b
    activ = jax.nn.gelu(pre, approximate=True).astype(BF16)
    mixed = sum_rows(dot(activ, down_w, ((1,), (0,))))
    result = middle + layer_norm(mixed, gain_d, shift_d)
    grad_mixed, grad_gain_d, grad_shift_d = norm_pull(mixed, gain_d, cotangent)
    grad_mixed = spread_rows(grad_mixed.astype(BF16))
    grad_activ = dot(grad_mixed, down_w, ((1,), (1,)))
    _, gelu_pull = jax.vjp(partial(jax.nn.gelu, approximate=True), pre)
    grad_pre = gelu_pull(grad_activ)[0].astype(BF16)
    grad_upbias = jnp.sum(grad_pre.astype(F32), 0)
    grad_inner = sum_rows(dot(grad_pre, up_w, ((1,), (1,))))
    grad_down = dot(activ, grad_mixed, ((0,), (0,)))
    grad_up = dot(inner, grad_pre, ((0,), (0,)))
    grad_side, grad_gain_c, grad_shift_c = norm_pull(middle, gain_c, grad_inner)
    grad_middle = cotangent + grad_side
    grad_branch, grad_gain_b, grad_shift_b = norm_pull(branch, gain_b, grad_middle)
    grad_branch = spread_rows(grad_branch.astype(BF16))
    grad_out = dot(attended, grad_branch, ((0,), (0,)))
    grad_attended = dot(grad_branch, out_w, ((1,), (1,))).astype(BF16)
    grad_triple = attend_pull(grad_attended)
    grad_qkv = dot(normed, grad_triple, ((0,), (0,)))
    grad_normed = sum_rows(dot(grad_triple, qkv_w, ((1,), (1,))))
    grad_first, grad_gain_a, grad_shift_a = norm_pull(inputs, gain_a, grad_normed)
    grad_inputs = grad_middle + grad_first
    small_grads = jnp.stack(
        [
            grad_gain_a,
            grad_shift_a,
            grad_gain_b,
            grad_shift_b,
            grad_gain_c,
            grad_shift_c,
            grad_gain_d,
            grad_shift_d,
        ]
    )
    small_grads = lax.psum_scatter(small_grads, ("seq", "fsdp"), scatter_dimension=1, tiled=True)
    grad_upbias = lax.psum_scatter(grad_upbias, "fsdp", scatter_dimension=0, tiled=True)
    return (
        result.astype(BF16)[None],
        grad_inputs[None],
        columns_back(grad_qkv, 3),
        rows_back(grad_out),
        columns_back(grad_up, 1),
        grad_upbias,
        rows_back(grad_down),
        small_grads[0],
        small_grads[1],
        small_grads[2],
        small_grads[3],
        small_grads[4],
        small_grads[5],
        small_grads[6],
        small_grads[7],
    )


def solution(mesh):
    rows = P(("seq", "fsdp"), None)
    vector = P(("seq", "fsdp"))
    acts = P("fsdp", "seq", None)
    placed = (acts, P("fsdp", "seq"), rows, rows, rows, vector, rows) + (vector,) * 8 + (acts,)
    return jax.shard_map(
        on_device,
        mesh=mesh,
        in_specs=placed,
        out_specs=(acts, acts, rows, rows, rows, vector, rows) + (vector,) * 8,
        check_vma=False,
    )
```

profile of v0, /device:TPU:0, one launch (start us, length us, event | category | flops | bytes accessed | tf_op | source)
XLA Modules:
  0.0 792.2 jit_solution(1543437263982148895)
XLA Ops:
  8.6 10.6 %all_to_all.20 = bf16[4,32,768]{2,1,0:T(8,128)(2,1)} all-to-all(bf16[4,32,768]{2,1,0:T(8,128)(2,1)S(1)} %reshape.212), channel_id=1, replica_groups=mesh['seq'=4,'fsdp'=8] {'seq'}, dimensions={0} | all-to-all | bytes 393216 | tf_op jit(solution)/shard_map/all_to_all | solution.py:93
  20.1 40.2 %all-gather.1 = bf16[32,32,8]{1,2,0:T(8,128)(2,1)S(1)} all-gather(bf16[1,32,8]{1,2,0:T(8,128)(2,1)S(1)} %bitcast.285), channel_id=1, replica_groups=mesh['seq'=4,'fsdp'=8] {'seq','fsdp'}, dimensions={0}, use_global_device_ids=true | all-gather | bytes 16896 | tf_op jit(solution)/shard_map/all_gather | solution.py:131
  63.0 2.1 fusion.70
  65.2 8.2 %all-gather = s32[1,1024]{1,0:T(1,128)S(1)} all-gather(s32[1,256]{1,0:T(1,128)S(1)} %copy-done.13), channel_id=2, replica_groups=mesh['seq'=4,'fsdp'=8] {'seq'}, dimensions={1}, use_global_device_ids=true | all-gather | bytes 5120 | tf_op jit(solution)/shard_map/all_gather | solution.py:118
  73.4 14.9 %all_gather.37 = bf16[256,1024]{1,0:T(8,128)(2,1)S(1)} all-gather(bf16[32,1024]{1,0:T(8,128)(2,1)S(1)} %copy-done.12), channel_id=1, replica_groups=mesh['seq'=4,'fsdp'=8] {'fsdp'}, dimensions={0}, use_global_device_ids=true | all-gather | bytes 589824 | tf_op jit(solution)/shard_map/all_gather | solution.py:134
  89.0 9.1 %all-gather.11.cloned.1.call-done = bf16[1024,1024]{1,0:T(8,128)(2,1)} async-done(((bf16[256,1024]{1,0:T(8,128)(2,1)}), bf16[1024,1024]{1,0:T(8,128)(2,1)}) %all-gather.11.cloned.1.call-update) | async-done | bytes 2097168 | tf_op jit(solution)/shard_map/all_gather | solution.py:111
  98.0 5.0 convolution_convert_fusion.7
  103.0 10.8 %fusion.94 = (f32[4,1024]{1,0:T(4,128)S(1)}, f32[4,1024,1024]{1,2,0:T(8,128)}) fusion(pred[1024,1024]{0,1:T(8,128)(4,1)S(1)} %fusion.16, bf16[1024,3,4,64]{0,3,2,1:T(8,128)(2,1)} %bitcast.243), kind=kOutput, calls=%fused_computation.151 | convolution fusion | flops 553649152 | bytes 18890752 | tf_op jit(solution)/shard_map/sub | solution.py:43
  113.8 7.5 fusion.38
  124.6 8.4 %all_to_all.21 = bf16[4,32,1024]{2,1,0:T(8,128)(2,1)S(1)} all-to-all(bf16[4,32,1024]{2,1,0:T(8,128)(2,1)S(1)} %copy.69), channel_id=1, replica_groups=mesh['seq'=4,'fsdp'=8] {'seq'}, dimensions={0} | all-to-all | bytes 524288 | tf_op jit(solution)/shard_map/all_to_all | solution.py:93
  134.1 25.5 %reduce-scatter.14.cloned.1.call-done = bf16[256,1024]{1,0:T(8,128)(2,1)} async-done(((bf16[1024,1024]{1,0:T(8,128)(2,1)}), bf16[256,1024]{1,0:T(8,128)(2,1)}) %reduce-scatter.14.cloned.1.call-update) | async-done | bytes 524304 | tf_op jit(solution)/shard_map/reduce_scatter | solution.py:114
  165.2 2.6 add_convert_fusion
  168.5 11.8 %all-gather.2 = bf16[8,1,128]{2,1,0:T(2,128)(2,1)S(1)} all-gather(bf16[1,1,128]{2,1,0:T(2,128)(2,1)S(1)} %bitcast.297), channel_id=1, replica_groups=mesh['seq'=4,'fsdp'=8] {'fsdp'}, dimensions={0}, use_global_device_ids=true | all-gather | bytes 2304 | tf_op jit(solution)/shard_map/all_gather | solution.py:136
  180.3 10.6 %all-gather.17.cloned.1.call-done = bf16[4,256,1024]{2,0,1:T(4,128)(2,1)} async-done(((bf16[4,32,1024]{2,0,1:T(4,128)(2,1)}), bf16[4,256,1024]{2,0,1:T(4,128)(2,1)}) %all-gather.17.cloned.1.call-update) | async-done | bytes 2097168 | tf_op jit(solution)/shard_map/all_gather | solution.py:94
  190.9 2.2 copy.71
  193.1 35.0 %all-gather.15.cloned.1.call-done = bf16[1024,1024]{1,0:T(8,128)(2,1)} async-done(((bf16[256,1024]{1,0:T(8,128)(2,1)}), bf16[1024,1024]{1,0:T(8,128)(2,1)}) %all-gather.15.cloned.1.call-update) | async-done | bytes 2097168 | tf_op jit(solution)/shard_map/all_gather | solution.py:111
  228.1 5.8 fusion.95
  234.0 24.8 %all-gather.19.cloned.1.call-done = bf16[1024,1024]{1,0:T(8,128)(2,1)} async-done(((bf16[128,1024]{1,0:T(8,128)(2,1)}), bf16[1024,1024]{1,0:T(8,128)(2,1)}) %all-gather.19.cloned.1.call-update) | async-done | bytes 2097168 | tf_op jit(solution)/shard_map/all_gather | solution.py:137
  258.8 7.1 convolution_convert_fusion.3
  265.9 34.8 %reduce-scatter.16.cloned.1.call-done = bf16[256,1024]{1,0:T(8,128)(2,1)} async-done(((bf16[1024,1024]{1,0:T(8,128)(2,1)}), bf16[256,1024]{1,0:T(8,128)(2,1)}) %reduce-scatter.16.cloned.1.call-update) | async-done | bytes 524304 | tf_op jit(solution)/shard_map/reduce_scatter | solution.py:114
  304.9 2.2 fusion.60
  307.4 35.2 %all-gather.21.cloned.1.call-done = bf16[1024,1024]{1,0:T(8,128)(2,1)} async-done(((bf16[256,1024]{1,0:T(8,128)(2,1)}), bf16[1024,1024]{1,0:T(8,128)(2,1)}) %all-gather.21.cloned.1.call-update) | async-done | bytes 2097168 | tf_op jit(solution)/shard_map/all_gather | solution.py:111
  342.6 7.3 convert_reduce_fusion
  351.2 5.4 convolution_convert_fusion.2
  356.7 35.3 %reduce-scatter.18.cloned.1.call-done = bf16[256,1024]{1,0:T(8,128)(2,1)} async-done(((bf16[1024,1024]{1,0:T(8,128)(2,1)}), bf16[256,1024]{1,0:T(8,128)(2,1)}) %reduce-scatter.18.cloned.1.call-update) | async-done | bytes 524304 | tf_op jit(solution)/shard_map/reduce_scatter | solution.py:114
  393.9 3.4 fusion.67
  398.5 6.0 convolution_convert_fusion.1
  405.0 28.9 %all-gather.23.cloned.1.call-done = bf16[1024,1024]{1,0:T(8,128)(2,1)} async-done(((bf16[256,1024]{1,0:T(8,128)(2,1)}), bf16[1024,1024]{1,0:T(8,128)(2,1)}) %all-gather.23.cloned.1.call-update) | async-done | bytes 2097168 | tf_op jit(solution)/shard_map/all_gather | solution.py:111
  433.9 2.5 convolution_convert_fusion.9
  437.2 9.6 %fusion.25 = bf16[1024,1,4,64]{0,3,2,1:T(8,128)(2,1)} fusion(bf16[1024,4,64]{0,2,1:T(8,128)(2,1)S(1)} %bitcast.308, f32[4,1024,1024]{1,2,0:T(8,128)} %get-tuple-element.51, f32[4,1024]{1,0:T(4,128)S(1)} %get-tuple-element.50), kind=kOutput, calls=%fused_computation.50 | convolution fusion | flops 545259520 | bytes 17842176 | tf_op jit(solution)/shard_map/hqk,qhd->khd/dot_general | solution.py:61
  446.9 9.4 %multiply_reduce_fusion = (f32[4,1024]{1,0:T(4,128)S(1)}, f32[4,1024,1024]{1,2,0:T(8,128)}) fusion(f32[4,1024,1024]{1,2,0:T(8,128)S(1)} %bitcast.229, f32[4,1024]{1,0:T(4,128)S(1)} %get-tuple-element.50, bf16[1024,4,64]{0,2,1:T(8,128)(2,1)} %bitcast.309, bf16[1024,3,4,64]{0,3,2,1:T(8,128)(2,1)} %bitcast.245), kind=kOutput, calls=%fused_computation.2 | convolution fusion | flops 549449728 | bytes 34635776 | tf_op jit(solution)/shard_map/qhd,khd->hqk/dot_general | solution.py:52
  456.3 7.9 %multiply_convert_fusion = bf16[4,1024,1024]{1,2,0:T(8,128)(2,1)S(1)} fusion(f32[4,1024,1024]{1,2,0:T(8,128)} %get-tuple-element.53, f32[4,1024]{1,0:T(4,128)S(1)} %get-tuple-element.52, f32[4,1024,1024]{1,2,0:T(8,128)S(1)} %bitcast.229, f32[4,1024]{1,0:T(4,128)S(1)} %get-tuple-element.50), kind=kLoop, calls=%fused_computation.1 | loop fusion | flops 16777216 | bytes 41975808 | tf_op jit(solution)/shard_map/convert_element_type | solution.py:54
  464.2 3.7 fusion.28
  467.9 2.8 fusion.29
  474.4 7.4 convolution_convert_fusion
  481.8 3.1 convolution_convert_fusion.8
  485.0 5.1 convolution_convert_fusion.5
  490.8 10.7 %all-reduce.4.cloned.1.call-done = bf16[8,4,32,1024]{3,2,0,1:T(8,128)(2,1)} async-done(((bf16[8,4,32,1024]{3,2,0,1:T(8,128)(2,1)}), bf16[8,4,32,1024]{3,2,0,1:T(8,128)(2,1)}) %all-reduce.4.cloned.1.call-update) | async-done | bytes 2097168
  501.4 2.3 dynamic-slice_bitcast_fusion
  503.7 3.6 all-to-all-start.3
  508.1 13.7 %all-reduce.1 = f32[1024]{0:T(1024)S(1)} all-reduce(f32[1024]{0:T(1024)S(1)} %get-tuple-element.30), channel_id=10, replica_groups=mesh['seq'=4,'fsdp'=8] {'fsdp'}, use_global_device_ids=true, to_apply=%region_27.28.clone | all-reduce | flops 1024 | bytes 8192
  522.4 15.0 %reduce-scatter.22.cloned.1.call-done = bf16[1,4,32,768]{3,2,1,0:T(8,128)(2,1)} async-done(((bf16[8,4,32,768]{3,2,1,0:T(8,128)(2,1)}), bf16[1,4,32,768]{3,2,1,0:T(8,128)(2,1)}) %reduce-scatter.22.cloned.1.call-update) | async-done | bytes 196624 | tf_op jit(solution)/shard_map/reduce_scatter | solution.py:100
  537.4 4.0 all-to-all-start.2
  542.9 31.2 %reduce-scatter.26.cloned.1.call-done = bf16[128,1024]{1,0:T(8,128)(2,1)} async-done(((bf16[1024,1024]{1,0:T(8,128)(2,1)}), bf16[128,1024]{1,0:T(8,128)(2,1)}) %reduce-scatter.26.cloned.1.call-update) | async-done | bytes 262160 | tf_op jit(solution)/shard_map/reduce_scatter | solution.py:106
  576.0 30.6 %reduce-scatter.24.cloned.1.call-done = bf16[32,1024]{1,0:T(8,128)(2,1)} async-done(((bf16[256,1024]{1,0:T(8,128)(2,1)}), bf16[32,1024]{1,0:T(8,128)(2,1)}) %reduce-scatter.24.cloned.1.call-update) | async-done | bytes 65552 | tf_op jit(solution)/shard_map/reduce_scatter | solution.py:106
  609.5 33.3 %reduce-scatter.20.cloned.1.call-done = bf16[256,1024]{1,0:T(8,128)(2,1)} async-done(((bf16[1024,1024]{1,0:T(8,128)(2,1)}), bf16[256,1024]{1,0:T(8,128)(2,1)}) %reduce-scatter.20.cloned.1.call-update) | async-done | bytes 524304 | tf_op jit(solution)/shard_map/reduce_scatter | solution.py:114
  645.5 2.4 fusion.74
  647.9 131.7 %reduce-scatter.28.cloned.1.call-done = f32[32,8]{1,0:T(8,128)} async-done(((f32[1024,8]{1,0:T(8,128)}), f32[32,8]{1,0:T(8,128)}) %reduce-scatter.28.cloned.1.call-update) | async-done | bytes 1040
  (149 shorter events, 46.0 us)
Async XLA Ops:
  7.2 58.0 %copy-start.13 = (s32[1,256]{1,0:T(1,128)S(1)}, s32[1,256]{1,0:T(1,128)}, u32[]{:S(2)}) copy-start(s32[1,256]{1,0:T(1,128)} %param.17) | copy-start | bytes 3076
  7.2 66.2 %copy-start.12 = (bf16[32,1024]{1,0:T(8,128)(2,1)S(1)}, bf16[32,1024]{1,0:T(8,128)(2,1)}, u32[]{:S(2)}) copy-start(bf16[32,1024]{1,0:T(8,128)(2,1)} %param.19) | copy-start | bytes 196612
  7.2 81.8 %all-gather.13.cloned.1.call-start = ((), (), s32[]{:S(2)}) async-start(), calls=%async_computation.13 | async-start | bytes 1769472 | tf_op jit(solution)/shard_map/all_gather | solution.py:94
  19.3 78.7 %all-gather.11.cloned.1.call-start = ((), (), s32[]{:S(2)}) async-start(), calls=%async_computation.12 | async-start | bytes 2621440 | tf_op jit(solution)/shard_map/all_gather | solution.py:111
  65.2 94.4 %reduce-scatter.14.cloned.1.call-start = ((), (), s32[]{:S(2)}) async-start(), calls=%async_computation.14 | async-start | bytes 2621440 | tf_op jit(solution)/shard_map/reduce_scatter | solution.py:114
  88.3 33.0 %copy-start.5 = (bf16[256,1024]{1,0:T(8,128)(2,1)}, bf16[256,1024]{1,0:T(8,128)(2,1)S(1)}, u32[]{:S(2)}) copy-start(bf16[256,1024]{1,0:T(8,128)(2,1)S(1)} %all_gather.37) | copy-start | bytes 1572868
  121.4 0.8 copy-start.8
  121.4 2.9 copy-start.11
  122.2 40.0 %copy-start = (bf16[1,256,1024]{2,1,0:T(8,128)(2,1)S(1)}, bf16[1,256,1024]{2,1,0:T(8,128)(2,1)}, u32[]{:S(2)}) copy-start(bf16[1,256,1024]{2,1,0:T(8,128)(2,1)} %param.16) | copy-start | bytes 1572868
  124.2 44.2 %copy-start.14 = (bf16[128]{0:T(256)(128)(2,1)S(1)}, bf16[128]{0:T(256)(128)(2,1)}, u32[]{:S(2)}) copy-start(bf16[128]{0:T(256)(128)(2,1)} %param.21) | copy-start | bytes 772
  124.2 66.6 %all-gather.17.cloned.1.call-start = ((), (), s32[]{:S(2)}) async-start(), calls=%async_computation.16 | async-start | bytes 2359296 | tf_op jit(solution)/shard_map/all_gather | solution.py:94
  133.9 94.2 %all-gather.15.cloned.1.call-start = ((), (), s32[]{:S(2)}) async-start(), calls=%async_computation.15 | async-start | bytes 2621440 | tf_op jit(solution)/shard_map/all_gather | solution.py:111
  167.8 90.9 %all-gather.19.cloned.1.call-start = ((), (), s32[]{:S(2)}) async-start(), calls=%async_computation.17 | async-start | bytes 2359296 | tf_op jit(solution)/shard_map/all_gather | solution.py:137
  168.4 132.3 %reduce-scatter.16.cloned.1.call-start = ((), (), s32[]{:S(2)}) async-start(), calls=%async_computation.18 | async-start | bytes 2621440 | tf_op jit(solution)/shard_map/reduce_scatter | solution.py:114
  193.1 40.9 %copy-start.4 = (bf16[4,256,1024]{2,1,0:T(8,128)(2,1)}, bf16[4,256,1024]{2,1,0:T(8,128)(2,1)S(1)}, u32[]{:S(2)}) copy-start(bf16[4,256,1024]{2,1,0:T(8,128)(2,1)S(1)} %copy.71) | copy-start | bytes 6291460
  258.8 44.5 %copy-start.3 = (bf16[1,256,1024]{2,1,0:T(8,128)(2,1)S(1)}, bf16[1,256,1024]{2,1,0:T(8,128)(2,1)}, u32[]{:S(2)}) copy-start(bf16[1,256,1024]{2,1,0:T(8,128)(2,1)} %param.31) | copy-start | bytes 1572868
  265.8 76.7 %copy-start.16 = (bf16[1024,1024]{1,0:T(8,128)(2,1)S(1)}, bf16[1024,1024]{1,0:T(8,128)(2,1)}, u32[]{:S(2)}) copy-start(bf16[1024,1024]{1,0:T(8,128)(2,1)} %all-gather.19.cloned.1.call-done) | copy-start | bytes 6291460
  265.9 76.7 %all-gather.21.cloned.1.call-start = ((), (), s32[]{:S(2)}) async-start(), calls=%async_computation.19 | async-start | bytes 2621440 | tf_op jit(solution)/shard_map/all_gather | solution.py:111
  307.1 84.9 %reduce-scatter.18.cloned.1.call-start = ((), (), s32[]{:S(2)}) async-start(), calls=%async_computation.20 | async-start | bytes 2621440 | tf_op jit(solution)/shard_map/reduce_scatter | solution.py:114
  349.9 1.3 copy-start.19
  351.2 40.8 %copy-start.1 = (bf16[256,1024]{1,0:T(8,128)(2,1)S(1)}, bf16[256,1024]{1,0:T(8,128)(2,1)}, u32[]{:S(2)}) copy-start(bf16[256,1024]{1,0:T(8,128)(2,1)} %reduce-scatter.14.cloned.1.call-done) | copy-start | bytes 1572868
  351.2 42.7 %copy-start.2 = (bf16[256,1024]{1,0:T(8,128)(2,1)S(1)}, bf16[256,1024]{1,0:T(8,128)(2,1)}, u32[]{:S(2)}) copy-start(bf16[256,1024]{1,0:T(8,128)(2,1)} %reduce-scatter.16.cloned.1.call-done) | copy-start | bytes 1572868
  356.6 77.3 %all-gather.23.cloned.1.call-start = ((), (), s32[]{:S(2)}) async-start(), calls=%async_computation.21 | async-start | bytes 2621440 | tf_op jit(solution)/shard_map/all_gather | solution.py:111
  398.4 35.5 %copy-start.6 = (bf16[256,1024]{1,0:T(8,128)(2,1)S(1)}, bf16[256,1024]{1,0:T(8,128)(2,1)}, u32[]{:S(2)}) copy-start(bf16[256,1024]{1,0:T(8,128)(2,1)} %copy-done.5) | copy-start | bytes 1572868
  398.5 103.0 %all-reduce.4.cloned.1.call-start = ((), (), s32[]{:S(2)}) async-start(), calls=%async_computation.27 | async-start | bytes 4194304
  404.6 132.8 %reduce-scatter.22.cloned.1.call-start = ((), (), s32[]{:S(2)}) async-start(), calls=%async_computation.23 | async-start | bytes 1769472 | tf_op jit(solution)/shard_map/reduce_scatter | solution.py:100
  433.9 12.9 %slice-start = ((s8[16777216]{0:T(1024)(128)(4,1)}), s8[4194304]{0:T(1024)(128)(4,1)S(1)}, s32[]{:S(2)}) async-start(s8[16777216]{0:T(1024)(128)(4,1)} %bitcast.228), calls=%async_computation.28 | async-start | bytes 8388608
  436.4 0.8 copy-start.17
  437.2 9.6 %slice-start.1 = ((s8[16777216]{0:T(1024)(128)(4,1)}), s8[4194304]{0:T(1024)(128)(4,1)S(1)}, s32[]{:S(2)}) async-start(s8[16777216]{0:T(1024)(128)(4,1)} %bitcast.228), calls=%async_computation.29 | async-start | bytes 8388608
  437.2 9.6 %slice-start.2 = ((s8[16777216]{0:T(1024)(128)(4,1)}), s8[4194304]{0:T(1024)(128)(4,1)S(1)}, s32[]{:S(2)}) async-start(s8[16777216]{0:T(1024)(128)(4,1)} %bitcast.228), calls=%async_computation.30 | async-start | bytes 8388608
  437.2 9.7 %slice-start.3 = ((s8[16777216]{0:T(1024)(128)(4,1)}), s8[4194304]{0:T(1024)(128)(4,1)S(1)}, s32[]{:S(2)}) async-start(s8[16777216]{0:T(1024)(128)(4,1)} %bitcast.228), calls=%async_computation.31 | async-start | bytes 8388608
  467.9 2.8 copy-start.10
  467.9 3.0 copy-start.15
  470.9 1.9 copy-start.7
  474.1 7.7 copy-start.9
  474.2 100.0 %reduce-scatter.26.cloned.1.call-start = ((), (), s32[]{:S(2)}) async-start(), calls=%async_computation.25 | async-start | bytes 2359296 | tf_op jit(solution)/shard_map/reduce_scatter | solution.py:106
  481.8 124.8 %reduce-scatter.24.cloned.1.call-start = ((), (), s32[]{:S(2)}) async-start(), calls=%async_computation.24 | async-start | bytes 589824 | tf_op jit(solution)/shard_map/reduce_scatter | solution.py:106
  485.0 5.2 copy-start.18
  485.0 157.8 %reduce-scatter.20.cloned.1.call-start = ((), (), s32[]{:S(2)}) async-start(), calls=%async_computation.22 | async-start | bytes 2621440 | tf_op jit(solution)/shard_map/reduce_scatter | solution.py:114
  503.7 18.7 %all-to-all-start.3 = ((bf16[4,32,1024]{2,1,0:T(8,128)(2,1)}), bf16[4,32,1024]{2,1,0:T(8,128)(2,1)S(1)}, u32[]{:S(2)}, u32[]{:S(2)}) async-start(bf16[4,32,1024]{2,1,0:T(8,128)(2,1)} %dynamic-slice_bitcast_fusion), calls=%async_computation.9 | async-start | bytes 524288 | tf_op jit(solution)/shard_map/all_to_all | solution.py:101
  537.4 70.7 %all-to-all-start.2 = ((bf16[4,32,768]{2,1,0:T(8,128)(2,1)}), bf16[4,32,768]{2,1,0:T(8,128)(2,1)S(1)}, u32[]{:S(2)}, u32[]{:S(2)}) async-start(bf16[4,32,768]{2,1,0:T(8,128)(2,1)} %bitcast.257), calls=%async_computation.7 | async-start | bytes 393216 | tf_op jit(solution)/shard_map/all_to_all | solution.py:101
  541.4 238.2 %reduce-scatter.28.cloned.1.call-start = ((), (), s32[]{:S(2)}) async-start(), calls=%async_computation.26 | async-start | bytes 540672
Sparse Core Ops, SparseCore 0:
  19.4 24.8 all-gather.12
  65.3 32.6 all-gather.10
  124.4 35.1 reduce-scatter.13
  161.7 29.1 all-gather.16
  193.3 34.7 all-gather.14
  229.6 29.0 all-gather.18
  266.0 34.6 reduce-scatter.15
  307.2 35.2 all-gather.20
  356.8 35.1 reduce-scatter.17
  398.6 35.2 all-gather.22
  436.4 64.9 all-reduce.3
  503.7 33.6 reduce-scatter.21
  539.8 34.2 reduce-scatter.25
  577.0 29.5 reduce-scatter.23
  609.4 33.3 reduce-scatter.19
  645.7 133.9 reduce-scatter.27
where the time goes:
time: 802 us; the launch traced here: 792 us
  waiting for transfers between devices  493 us (61%)
  blocking collectives  108 us (13%)
  matrix products  102 us (13%)
  other arithmetic  41.7 us (5%)
  local copies, waits for them, and re-layouts  23.2 us (3%)
  between operations  15.3 us (2%)
  starting transfers between devices  9.24 us (1%)
    unnamed x18, waiting for transfers between devices  143 us
    reduce_scatter x4, waiting for transfers between devices, sum_rows(): lax.psum_scatter(value.astype(BF16), 'seq', scatter_dimension=0, tiled=True)  129 us
    all_gather x4, waiting for transfers between devices, spread_rows(): return lax.all_gather(value, 'seq', axis=0, tiled=True)  108 us
    reduce_scatter x2, waiting for transfers between devices, rows_back(): lax.psum_scatter(grad.astype(BF16), 'fsdp', scatter_dimension=0, tiled=True)  61.9 us
    dot_general x12, matrix products, dot(): lax.dot_general(left, right, (dims, ((), ())), preferred_element_type=F32)  58.7 us
    all_gather x1, blocking collectives, on_device(): lax.all_gather(small, ('seq', 'fsdp'), axis=1, tiled=True).astype(F32)  40.2 us
    all_gather x1, waiting for transfers between devices, on_device(): down_w = lax.all_gather(down_weight, 'fsdp', axis=0, tiled=True)  24.8 us
    all_to_all x2, blocking collectives, columns(): cut = lax.all_to_all(cut, 'seq', split_axis=0, concat_axis=0, tiled=True)  19 us
  transfers between devices with their start and end apart: 18, of which 15 were waited for; matrix products, arithmetic and copies ran while one was open for 12% of the time, Pallas kernels for 0%

commit v1 on v0

--- a/solution.py
+++ b/solution.py
@@ -7,6 +7,28 @@
 HEAD_DIM = 64
 F32 = jnp.float32
 BF16 = jnp.bfloat16
+
+
+def joined_along(parts, dim):
+    parts = jnp.moveaxis(parts, 0, dim)
+    dims = parts.shape
+    return parts.reshape(*dims[:dim], dims[dim] * dims[dim + 1], *dims[dim + 2 :])
+
+
+def grow_blocks(x, axis):
+    size = lax.axis_size(axis)
+    tiles = x[None]
+    for level in range(size.bit_length() - 1):
+        distance = 1 << level
+        partner_block = lax.ppermute(tiles, axis, [(i, i ^ distance) for i in range(size)])
+        both = jnp.stack([tiles, partner_block])
+        upper = lax.axis_index(axis) >> level & 1
+        tiles = jnp.where(upper == 0, both, both[::-1]).reshape(-1, *x.shape)
+    return tiles
+
+
+def collect(array, axis, dim):
+    return joined_along(grow_blocks(array, axis), dim)
 
 
 def layer_norm(value, gain, shift):
@@ -108,7 +130,7 @@
         )
 
     def spread_rows(value):
-        return lax.all_gather(value, "seq", axis=0, tiled=True)
+        return collect(value, "seq", 0)
 
     def sum_rows(value):
         return lax.psum_scatter(value.astype(BF16), "seq", scatter_dimension=0, tiled=True).astype(

time: 802 us -> 768 us (0.958)
  waiting for transfers between devices: 493 us -> 425 us
  blocking collectives: 108 us -> 122 us
  starting transfers between devices: 9.24 us -> 23.2 us
  matrix products: 102 us -> 91.6 us
  local copies, waits for them, and re-layouts: 23.2 us -> 31.4 us
    all_gather x4 -> x0, waiting for transfers between devices: 108 us -> none  [spread_rows(): return lax.all_gather(value, 'seq', axis=0, tiled=True)]
    ppermute x0 -> x8, waiting for transfers between devices: none -> 99.5 us  [grow_blocks(): lax.ppermute(tiles, axis, [(i, i ^ distance) for i in range(size)])]
    all_gather x1, blocking collectives: 8.18 us -> 26.4 us  [on_device(): segment_all = lax.all_gather(segments[0], 'seq', axis=0, tiled=True)]
    reduce_scatter x1, waiting for transfers between devices: 15 us -> 0.01 us  [columns_back(): cut = lax.psum_scatter(cut, 'fsdp', scatter_dimension=0, tiled=True)[0]]
    all_gather x1, waiting for transfers between devices: 24.8 us -> 10.1 us  [on_device(): down_w = lax.all_gather(down_weight, 'fsdp', axis=0, tiled=True)]
    all_gather x2, waiting for transfers between devices: 10.6 us -> 0.02 us  [columns(): whole = lax.all_gather(cut, 'fsdp', axis=1, tiled=True)]
    unnamed x18 -> x14, waiting for transfers between devices: 143 us -> 133 us
    ppermute x0 -> x8, starting transfers between devices: none -> 9.52 us  [grow_blocks(): lax.ppermute(tiles, axis, [(i, i ^ distance) for i in range(size)])]
  transfers between devices with their start and end apart: 18 -> 23, of which waited for: 15 -> 15; matrix products, arithmetic and copies ran while one was open for 12% -> 12% of each run, Pallas kernels for 0% -> 0%
where the time goes in v1:
time: 768 us; the launch traced here: 758 us
  waiting for transfers between devices  425 us (55%)
  blocking collectives  122 us (16%)
  matrix products  91.6 us (12%)
  other arithmetic  48.6 us (6%)
  local copies, waits for them, and re-layouts  31.4 us (4%)
  starting transfers between devices  23.2 us (3%)
  between operations  15.9 us (2%)
    unnamed x14, waiting for transfers between devices  133 us
    reduce_scatter x4, waiting for transfers between devices, sum_rows(): lax.psum_scatter(value.astype(BF16), 'seq', scatter_dimension=0, tiled=True)  123 us
    ppermute x8, waiting for transfers between devices, grow_blocks(): lax.ppermute(tiles, axis, [(i, i ^ distance) for i in range(size)])  99.5 us
    reduce_scatter x2, waiting for transfers between devices, rows_back(): lax.psum_scatter(grad.astype(BF16), 'fsdp', scatter_dimension=0, tiled=True)  59.6 us
    dot_general x12, matrix products, dot(): lax.dot_general(left, right, (dims, ((), ())), preferred_element_type=F32)  49.3 us
    all_gather x1, blocking collectives, on_device(): lax.all_gather(small, ('seq', 'fsdp'), axis=1, tiled=True).astype(F32)  42.5 us
    all_gather x1, blocking collectives, on_device(): segment_all = lax.all_gather(segments[0], 'seq', axis=0, tiled=True)  26.4 us
    unnamed x100, local copies, waits for them, and re-layouts  19.2 us
  transfers between devices with their start and end apart: 23, of which 15 were waited for; matrix products, arithmetic and copies ran while one was open for 12% of the time, Pallas kernels for 0%

profile of v1, /device:TPU:0, one launch (start us, length us, event | category | flops | bytes accessed | tf_op | source)
XLA Modules:
  0.0 757.9 jit_solution(2444941821536806892)
XLA Ops:
  9.4 5.2 all-to-all-start
  15.9 42.5 %all-gather.1 = bf16[32,32,8]{1,2,0:T(8,128)(2,1)S(1)} all-gather(bf16[1,32,8]{1,2,0:T(8,128)(2,1)S(1)} %bitcast.372), channel_id=1, replica_groups=mesh['seq'=4,'fsdp'=8] {'seq','fsdp'}, dimensions={0}, use_global_device_ids=true | all-gather | bytes 16896 | tf_op jit(solution)/shard_map/all_gather | solution.py:153
  60.3 13.9 %collective-permute-done = bf16[1,256,1024]{2,1,0:T(8,128)(2,1)S(1)} collective-permute-done((bf16[1,256,1024]{2,1,0:T(8,128)(2,1)S(1)}, bf16[1,256,1024]{2,1,0:T(8,128)(2,1)S(1)}, u32[]{:S(2)}, u32[]{:S(2)}) %collective-permute-start) | collective-permute-done | bytes 524320 | tf_op jit(solution)/shard_map/ppermute | solution.py:23
  75.4 26.4 %all-gather = s32[1,1024]{1,0:T(1,128)S(1)} all-gather(s32[1,256]{1,0:T(1,128)S(1)} %copy-done.29), channel_id=2, replica_groups=mesh['seq'=4,'fsdp'=8] {'seq'}, dimensions={1}, use_global_device_ids=true | all-gather | bytes 5120 | tf_op jit(solution)/shard_map/all_gather | solution.py:140
  101.8 15.0 %all_gather.24 = bf16[256,1024]{1,0:T(8,128)(2,1)S(1)} all-gather(bf16[32,1024]{1,0:T(8,128)(2,1)S(1)} %copy-done.24), channel_id=1, replica_groups=mesh['seq'=4,'fsdp'=8] {'fsdp'}, dimensions={0}, use_global_device_ids=true | all-gather | bytes 589824 | tf_op jit(solution)/shard_map/all_gather | solution.py:156
  120.4 5.2 convolution_convert_fusion.7
  125.7 11.1 %fusion.114 = (f32[4,1024]{1,0:T(4,128)S(1)}, f32[4,1024,1024]{1,2,0:T(8,128)}) fusion(pred[1024,1024]{0,1:T(8,128)(4,1)} %fusion.16, bf16[1024,3,4,64]{0,3,2,1:T(8,128)(2,1)} %bitcast.318), kind=kOutput, calls=%fused_computation.187 | convolution fusion | flops 553649152 | bytes 18890752 | tf_op jit(solution)/shard_map/sub | solution.py:65
  136.8 7.5 fusion.33
  145.1 2.1 convolution_convert_fusion.4
  147.6 11.4 %all_to_all.20 = bf16[4,32,1024]{2,1,0:T(8,128)(2,1)S(1)} all-to-all(bf16[4,32,1024]{2,1,0:T(8,128)(2,1)S(1)} %copy.87), channel_id=1, replica_groups=mesh['seq'=4,'fsdp'=8] {'seq'}, dimensions={0} | all-to-all | bytes 524288 | tf_op jit(solution)/shard_map/all_to_all | solution.py:115
  160.6 19.5 %reduce-scatter.14.cloned.1.call-done = bf16[256,1024]{1,0:T(8,128)(2,1)} async-done(((bf16[1024,1024]{1,0:T(8,128)(2,1)}), bf16[256,1024]{1,0:T(8,128)(2,1)}) %reduce-scatter.14.cloned.1.call-update) | async-done | bytes 524304 | tf_op jit(solution)/shard_map/reduce_scatter | solution.py:136
  187.2 11.8 %collective-permute-done.2 = bf16[1,256,1024]{2,1,0:T(8,128)(2,1)S(1)} collective-permute-done((bf16[1,256,1024]{2,1,0:T(8,128)(2,1)S(1)}, bf16[1,256,1024]{2,1,0:T(8,128)(2,1)S(1)}, u32[]{:S(2)}, u32[]{:S(2)}) %collective-permute-start.2) | collective-permute-done | bytes 524320 | tf_op jit(solution)/shard_map/ppermute | solution.py:23
  201.0 11.7 %all-gather.2 = bf16[8,1,128]{2,1,0:T(2,128)(2,1)S(1)} all-gather(bf16[1,1,128]{2,1,0:T(2,128)(2,1)S(1)} %bitcast.384), channel_id=1, replica_groups=mesh['seq'=4,'fsdp'=8] {'fsdp'}, dimensions={0}, use_global_device_ids=true | all-gather | bytes 2304 | tf_op jit(solution)/shard_map/all_gather | solution.py:158
  212.7 2.2 copy.89
  215.0 8.8 %collective-permute-done.3 = bf16[2,256,1024]{2,1,0:T(8,128)(2,1)} collective-permute-done((bf16[2,256,1024]{2,1,0:T(8,128)(2,1)S(1)}, bf16[2,256,1024]{2,1,0:T(8,128)(2,1)}, u32[]{:S(2)}, u32[]{:S(2)}) %collective-permute-start.3) | collective-permute-done | bytes 1048608 | tf_op jit(solution)/shard_map/ppermute | solution.py:23
  227.2 4.4 fusion.115
  231.5 10.1 %all-gather.11.cloned.1.call-done = bf16[1024,1024]{1,0:T(8,128)(2,1)} async-done(((bf16[128,1024]{1,0:T(8,128)(2,1)}), bf16[1024,1024]{1,0:T(8,128)(2,1)}) %all-gather.11.cloned.1.call-update) | async-done | bytes 2097168 | tf_op jit(solution)/shard_map/all_gather | solution.py:159
  241.7 7.0 convolution_convert_fusion.3
  249.0 34.6 %reduce-scatter.16.cloned.1.call-done = bf16[256,1024]{1,0:T(8,128)(2,1)} async-done(((bf16[1024,1024]{1,0:T(8,128)(2,1)}), bf16[256,1024]{1,0:T(8,128)(2,1)}) %reduce-scatter.16.cloned.1.call-update) | async-done | bytes 524304 | tf_op jit(solution)/shard_map/reduce_scatter | solution.py:136
  290.1 11.9 %collective-permute-done.4 = bf16[1,256,1024]{2,1,0:T(8,128)(2,1)S(1)} collective-permute-done((bf16[1,256,1024]{2,1,0:T(8,128)(2,1)S(1)}, bf16[1,256,1024]{2,1,0:T(8,128)(2,1)S(1)}, u32[]{:S(2)}, u32[]{:S(2)}) %collective-permute-start.4) | collective-permute-done | bytes 524320 | tf_op jit(solution)/shard_map/ppermute | solution.py:23
  303.8 22.6 %collective-permute-done.5 = bf16[2,256,1024]{2,1,0:T(8,128)(2,1)S(1)} collective-permute-done((bf16[2,256,1024]{2,1,0:T(8,128)(2,1)S(1)}, bf16[2,256,1024]{2,1,0:T(8,128)(2,1)S(1)}, u32[]{:S(2)}, u32[]{:S(2)}) %collective-permute-start.5) | collective-permute-done | bytes 1048608 | tf_op jit(solution)/shard_map/ppermute | solution.py:23
  327.2 2.1 copy-done.41
  330.1 5.1 convert_reduce_fusion
  336.5 3.7 convolution_convert_fusion.2
  340.3 35.3 %reduce-scatter.18.cloned.1.call-done = bf16[256,1024]{1,0:T(8,128)(2,1)} async-done(((bf16[1024,1024]{1,0:T(8,128)(2,1)}), bf16[256,1024]{1,0:T(8,128)(2,1)}) %reduce-scatter.18.cloned.1.call-update) | async-done | bytes 524304 | tf_op jit(solution)/shard_map/reduce_scatter | solution.py:136
  375.6 1.9 fusion.84
  377.5 3.4 fusion.76
  383.1 11.9 %collective-permute-done.6 = bf16[1,256,1024]{2,1,0:T(8,128)(2,1)S(1)} collective-permute-done((bf16[1,256,1024]{2,1,0:T(8,128)(2,1)S(1)}, bf16[1,256,1024]{2,1,0:T(8,128)(2,1)S(1)}, u32[]{:S(2)}, u32[]{:S(2)}) %collective-permute-start.6) | collective-permute-done | bytes 524320 | tf_op jit(solution)/shard_map/ppermute | solution.py:23
  398.2 3.7 convolution_convert_fusion.1
  402.4 18.7 %collective-permute-done.7 = bf16[2,256,1024]{2,1,0:T(8,128)(2,1)} collective-permute-done((bf16[2,256,1024]{2,1,0:T(8,128)(2,1)}, bf16[2,256,1024]{2,1,0:T(8,128)(2,1)}, u32[]{:S(2)}, u32[]{:S(2)}) %collective-permute-start.7) | collective-permute-done | bytes 1048608 | tf_op jit(solution)/shard_map/ppermute | solution.py:23
  424.5 8.7 %fusion.54 = bf16[1024,1,4,64]{0,3,2,1:T(8,128)(2,1)S(1)} fusion(bf16[1024,4,64]{0,2,1:T(8,128)(2,1)S(1)} %bitcast.395, f32[4,1024,1024]{1,2,0:T(8,128)} %get-tuple-element.59, f32[4,1024]{1,0:T(4,128)S(1)} %get-tuple-element.58), kind=kOutput, calls=%fused_computation.101 | convolution fusion | flops 545521664 | bytes 17842176 | tf_op jit(solution)/shard_map/hqk,qhd->khd/dot_general | solution.py:83
  433.2 10.7 %multiply_reduce_fusion = (f32[4,1024]{1,0:T(4,128)S(1)}, f32[4,1024,1024]{1,2,0:T(8,128)}) fusion(f32[4,1024,1024]{1,2,0:T(8,128)} %get-tuple-element.59, f32[4,1024]{1,0:T(4,128)S(1)} %get-tuple-element.58, bf16[1024,4,64]{0,2,1:T(8,128)(2,1)S(1)} %bitcast.396, bf16[1024,3,4,64]{0,3,2,1:T(8,128)(2,1)S(1)} %bitcast.320), kind=kOutput, calls=%fused_computation.2 | convolution fusion | flops 549449728 | bytes 34635776 | tf_op jit(solution)/shard_map/qhd,khd->hqk/dot_general | solution.py:74
  443.9 11.9 %multiply_convert_fusion = bf16[4,1024,1024]{1,2,0:T(8,128)(2,1)S(1)} fusion(f32[4,1024,1024]{1,2,0:T(8,128)} %get-tuple-element.61, f32[4,1024]{1,0:T(4,128)S(1)} %get-tuple-element.60, f32[4,1024,1024]{1,2,0:T(8,128)} %get-tuple-element.59, f32[4,1024]{1,0:T(4,128)S(1)} %get-tuple-element.58), kind=kLoop, calls=%fused_computation.1 | loop fusion | flops 16777216 | bytes 41975808 | tf_op jit(solution)/shard_map/convert_element_type | solution.py:76
  455.7 2.7 fusion.57
  460.2 2.0 copy-done.6
  462.2 1.9 convolution_convert_fusion.6
  465.6 7.2 convolution_convert_fusion
  473.8 3.2 convolution_convert_fusion.8
  477.1 5.0 convolution_convert_fusion.5
  483.4 2.3 dynamic-slice_bitcast_fusion
  485.7 3.4 all-to-all-start.3
  489.8 14.7 %all-reduce.1 = f32[1024]{0:T(1024)S(1)} all-reduce(f32[1024]{0:T(1024)S(1)} %get-tuple-element.30), channel_id=10, replica_groups=mesh['seq'=4,'fsdp'=8] {'fsdp'}, use_global_device_ids=true, to_apply=%region_27.28.clone | all-reduce | flops 1024 | bytes 8192
  505.2 3.9 all-to-all-start.2
  510.6 29.0 %reduce-scatter.26.cloned.1.call-done = bf16[128,1024]{1,0:T(8,128)(2,1)} async-done(((bf16[1024,1024]{1,0:T(8,128)(2,1)}), bf16[128,1024]{1,0:T(8,128)(2,1)}) %reduce-scatter.26.cloned.1.call-update) | async-done | bytes 262160 | tf_op jit(solution)/shard_map/reduce_scatter | solution.py:128
  539.5 1.8 convert_element_type.209
  541.3 30.6 %reduce-scatter.24.cloned.1.call-done = bf16[32,1024]{1,0:T(8,128)(2,1)} async-done(((bf16[256,1024]{1,0:T(8,128)(2,1)}), bf16[32,1024]{1,0:T(8,128)(2,1)}) %reduce-scatter.24.cloned.1.call-update) | async-done | bytes 65552 | tf_op jit(solution)/shard_map/reduce_scatter | solution.py:128
  574.8 33.4 %reduce-scatter.20.cloned.1.call-done = bf16[256,1024]{1,0:T(8,128)(2,1)} async-done(((bf16[1024,1024]{1,0:T(8,128)(2,1)}), bf16[256,1024]{1,0:T(8,128)(2,1)}) %reduce-scatter.20.cloned.1.call-update) | async-done | bytes 524304 | tf_op jit(solution)/shard_map/reduce_scatter | solution.py:136
  612.4 132.6 %reduce-scatter.28.cloned.1.call-done = f32[32,8]{1,0:T(8,128)} async-done(((f32[1024,8]{1,0:T(8,128)}), f32[32,8]{1,0:T(8,128)}) %reduce-scatter.28.cloned.1.call-update) | async-done | bytes 1040
  (213 shorter events, 66.2 us)
Async XLA Ops:
  7.2 51.4 %copy-start = (bf16[1,256,1024]{2,1,0:T(8,128)(2,1)S(1)}, bf16[1,256,1024]{2,1,0:T(8,128)(2,1)}, u32[]{:S(2)}) copy-start(bf16[1,256,1024]{2,1,0:T(8,128)(2,1)} %param.16) | copy-start | bytes 1572868
  7.2 8.6 %copy-start.37 = (bf16[32]{0:T(256)(128)(2,1)S(1)}, bf16[32]{0:T(256)(128)(2,1)}, u32[]{:S(2)}) copy-start(bf16[32]{0:T(256)(128)(2,1)} %param.30) | copy-start | bytes 196
  7.2 8.6 %copy-start.36 = (bf16[32]{0:T(256)(128)(2,1)S(1)}, bf16[32]{0:T(256)(128)(2,1)}, u32[]{:S(2)}) copy-start(bf16[32]{0:T(256)(128)(2,1)} %param.29) | copy-start | bytes 196
  7.2 8.6 %copy-start.35 = (bf16[32]{0:T(256)(128)(2,1)S(1)}, bf16[32]{0:T(256)(128)(2,1)}, u32[]{:S(2)}) copy-start(bf16[32]{0:T(256)(128)(2,1)} %param.28) | copy-start | bytes 196
  7.2 8.6 %copy-start.34 = (bf16[32]{0:T(256)(128)(2,1)S(1)}, bf16[32]{0:T(256)(128)(2,1)}, u32[]{:S(2)}) copy-start(bf16[32]{0:T(256)(128)(2,1)} %param.27) | copy-start | bytes 196
  7.2 8.6 %copy-start.33 = (bf16[32]{0:T(256)(128)(2,1)S(1)}, bf16[32]{0:T(256)(128)(2,1)}, u32[]{:S(2)}) copy-start(bf16[32]{0:T(256)(128)(2,1)} %param.26) | copy-start | bytes 196
  7.2 8.6 %copy-start.32 = (bf16[32]{0:T(256)(128)(2,1)S(1)}, bf16[32]{0:T(256)(128)(2,1)}, u32[]{:S(2)}) copy-start(bf16[32]{0:T(256)(128)(2,1)} %param.25) | copy-start | bytes 196
  7.3 8.6 %copy-start.31 = (bf16[32]{0:T(256)(128)(2,1)S(1)}, bf16[32]{0:T(256)(128)(2,1)}, u32[]{:S(2)}) copy-start(bf16[32]{0:T(256)(128)(2,1)} %param.24) | copy-start | bytes 196
  7.3 8.6 %copy-start.30 = (bf16[32]{0:T(256)(128)(2,1)S(1)}, bf16[32]{0:T(256)(128)(2,1)}, u32[]{:S(2)}) copy-start(bf16[32]{0:T(256)(128)(2,1)} %param.23) | copy-start | bytes 196
  9.4 49.5 %all-to-all-start = ((bf16[4,32,768]{2,1,0:T(8,128)(2,1)}), bf16[4,32,768]{2,1,0:T(8,128)(2,1)S(1)}, u32[]{:S(2)}, u32[]{:S(2)}) async-start(bf16[4,32,768]{2,1,0:T(8,128)(2,1)} %reshape.367), calls=%async_computation | async-start | bytes 393216 | tf_op jit(solution)/shard_map/all_to_all | solution.py:115
  14.6 105.8 %all-gather.7.cloned.1.call-start = ((), (), s32[]{:S(2)}) async-start(), calls=%async_computation.12 | async-start | bytes 1769472 | tf_op jit(solution)/shard_map/all_gather | solution.py:116
  15.8 58.4 %copy-start.25 = (f32[256]{0:T(256)}, f32[256]{0:T(256)S(1)}, u32[]{:S(2)}) copy-start(f32[256]{0:T(256)S(1)} %broadcast_multiply_fusion.11) | copy-start | bytes 3076
  58.6 15.6 %copy-start.22 = (f32[1,1024]{1,0:T(1,128)}, f32[1,1024]{1,0:T(1,128)S(1)}, u32[]{:S(2)}) copy-start(f32[1,1024]{1,0:T(1,128)S(1)} %get-tuple-element.49) | copy-start | bytes 12292
  59.6 120.5 %reduce-scatter.14.cloned.1.call-start = ((), (), s32[]{:S(2)}) async-start(), calls=%async_computation.13 | async-start | bytes 2621440 | tf_op jit(solution)/shard_map/reduce_scatter | solution.py:136
  59.7 14.5 %copy-start.27 = (f32[256]{0:T(256)}, f32[256]{0:T(256)S(1)}, u32[]{:S(2)}) copy-start(f32[256]{0:T(256)S(1)} %add_rsqrt_fusion.3) | copy-start | bytes 3076
  60.0 14.2 %collective-permute-start = (bf16[1,256,1024]{2,1,0:T(8,128)(2,1)S(1)}, bf16[1,256,1024]{2,1,0:T(8,128)(2,1)S(1)}, u32[]{:S(2)}, u32[]{:S(2)}) collective-permute-start(bf16[1,256,1024]{2,1,0:T(8,128)(2,1)S(1)} %fusion.89), channel_id=1, source_target_pairs={{0,8},{8,0},{16,24},{24,16},{1,9},{9,1},{17,25},{25,17},{2,10},{10... | collective-permute-start | bytes 1572872 | tf_op jit(solution)/shard_map/ppermute | solution.py:23
  74.3 27.5 %copy-start.24 = (bf16[32,1024]{1,0:T(8,128)(2,1)S(1)}, bf16[32,1024]{1,0:T(8,128)(2,1)}, u32[]{:S(2)}) copy-start(bf16[32,1024]{1,0:T(8,128)(2,1)} %param.19) | copy-start | bytes 196612
  74.7 43.7 %collective-permute-start.1 = (bf16[2,256,1024]{2,1,0:T(8,128)(2,1)S(1)}, bf16[2,256,1024]{2,1,0:T(8,128)(2,1)}, u32[]{:S(2)}, u32[]{:S(2)}) collective-permute-start(bf16[2,256,1024]{2,1,0:T(8,128)(2,1)S(1)} %get-tuple-element.41), channel_id=1, source_target_pairs={{0,16},{8,24},{16,0},{24,8},{1,17},{9,25},{17,1},{25,9},{2,18},{10... | collective-permute-start | bytes 3145736 | tf_op jit(solution)/shard_map/ppermute | solution.py:23
  116.8 27.5 %copy-start.13 = (bf16[256,1024]{1,0:T(8,128)(2,1)}, bf16[256,1024]{1,0:T(8,128)(2,1)S(1)}, u32[]{:S(2)}) copy-start(bf16[256,1024]{1,0:T(8,128)(2,1)S(1)} %all_gather.24) | copy-start | bytes 1572868
  120.4 5.3 copy-start.5
  147.2 65.5 %all-gather.9.cloned.1.call-start = ((), (), s32[]{:S(2)}) async-start(), calls=%async_computation.14 | async-start | bytes 2359296 | tf_op jit(solution)/shard_map/all_gather | solution.py:116
  159.9 81.7 %all-gather.11.cloned.1.call-start = ((), (), s32[]{:S(2)}) async-start(), calls=%async_computation.15 | async-start | bytes 2359296 | tf_op jit(solution)/shard_map/all_gather | solution.py:159
  160.5 123.1 %reduce-scatter.16.cloned.1.call-start = ((), (), s32[]{:S(2)}) async-start(), calls=%async_computation.16 | async-start | bytes 2621440 | tf_op jit(solution)/shard_map/reduce_scatter | solution.py:136
  185.2 13.7 %collective-permute-start.2 = (bf16[1,256,1024]{2,1,0:T(8,128)(2,1)S(1)}, bf16[1,256,1024]{2,1,0:T(8,128)(2,1)S(1)}, u32[]{:S(2)}, u32[]{:S(2)}) collective-permute-start(bf16[1,256,1024]{2,1,0:T(8,128)(2,1)S(1)} %fusion.147), channel_id=1, source_target_pairs={{0,8},{8,0},{16,24},{24,16},{1,9},{9,1},{17,25},{25,17},{2,10},{10... | collective-permute-start | bytes 1572872 | tf_op jit(solution)/shard_map/ppermute | solution.py:23
  199.5 24.3 %collective-permute-start.3 = (bf16[2,256,1024]{2,1,0:T(8,128)(2,1)S(1)}, bf16[2,256,1024]{2,1,0:T(8,128)(2,1)}, u32[]{:S(2)}, u32[]{:S(2)}) collective-permute-start(bf16[2,256,1024]{2,1,0:T(8,128)(2,1)S(1)} %get-tuple-element.39), channel_id=1, source_target_pairs={{0,16},{8,24},{16,0},{24,8},{1,17},{9,25},{17,1},{25,9},{2,18},{10... | collective-permute-start | bytes 3145736 | tf_op jit(solution)/shard_map/ppermute | solution.py:23
  214.9 10.9 %copy-start.10 = (bf16[4,256,1024]{2,1,0:T(8,128)(2,1)}, bf16[4,256,1024]{2,1,0:T(8,128)(2,1)S(1)}, u32[]{:S(2)}) copy-start(bf16[4,256,1024]{2,1,0:T(8,128)(2,1)S(1)} %copy.89) | copy-start | bytes 6291460
  248.7 37.5 %copy-start.3 = (bf16[1,256,1024]{2,1,0:T(8,128)(2,1)S(1)}, bf16[1,256,1024]{2,1,0:T(8,128)(2,1)}, u32[]{:S(2)}) copy-start(bf16[1,256,1024]{2,1,0:T(8,128)(2,1)} %param.31) | copy-start | bytes 1572868
  248.7 126.8 %reduce-scatter.18.cloned.1.call-start = ((), (), s32[]{:S(2)}) async-start(), calls=%async_computation.17 | async-start | bytes 2621440 | tf_op jit(solution)/shard_map/reduce_scatter | solution.py:136
  283.6 4.2 copy-start.2
  288.2 13.7 %collective-permute-start.4 = (bf16[1,256,1024]{2,1,0:T(8,128)(2,1)S(1)}, bf16[1,256,1024]{2,1,0:T(8,128)(2,1)S(1)}, u32[]{:S(2)}, u32[]{:S(2)}) collective-permute-start(bf16[1,256,1024]{2,1,0:T(8,128)(2,1)S(1)} %fusion.145), channel_id=1, source_target_pairs={{0,8},{8,0},{16,24},{24,16},{1,9},{9,1},{17,25},{25,17},{2,10},{10... | collective-permute-start | bytes 1572872 | tf_op jit(solution)/shard_map/ppermute | solution.py:23
  302.3 24.1 %collective-permute-start.5 = (bf16[2,256,1024]{2,1,0:T(8,128)(2,1)S(1)}, bf16[2,256,1024]{2,1,0:T(8,128)(2,1)S(1)}, u32[]{:S(2)}, u32[]{:S(2)}) collective-permute-start(bf16[2,256,1024]{2,1,0:T(8,128)(2,1)S(1)} %get-tuple-element.37), channel_id=1, source_target_pairs={{0,16},{8,24},{16,0},{24,8},{1,17},{9,25},{17,1},{25,9},{2,18},{10... | collective-permute-start | bytes 3145736 | tf_op jit(solution)/shard_map/ppermute | solution.py:23
  327.2 8.0 %copy-start.9 = (bf16[2,2,256,1024]{3,2,1,0:T(8,128)(2,1)}, bf16[2,2,256,1024]{3,2,1,0:T(8,128)(2,1)S(1)}, u32[]{:S(2)}) copy-start(bf16[2,2,256,1024]{3,2,1,0:T(8,128)(2,1)S(1)} %reverse_select_fusion.1) | copy-start | bytes 6291460
  330.1 6.4 copy-start.11
  340.2 143.1 %all-reduce.4.cloned.1.call-start = ((), (), s32[]{:S(2)}) async-start(), calls=%async_computation.23 | async-start | bytes 4194304
  381.2 13.7 %collective-permute-start.6 = (bf16[1,256,1024]{2,1,0:T(8,128)(2,1)S(1)}, bf16[1,256,1024]{2,1,0:T(8,128)(2,1)S(1)}, u32[]{:S(2)}, u32[]{:S(2)}) collective-permute-start(bf16[1,256,1024]{2,1,0:T(8,128)(2,1)S(1)} %fusion.143), channel_id=1, source_target_pairs={{0,8},{8,0},{16,24},{24,16},{1,9},{9,1},{17,25},{25,17},{2,10},{10... | collective-permute-start | bytes 1572872 | tf_op jit(solution)/shard_map/ppermute | solution.py:23
  396.8 24.3 %collective-permute-start.7 = (bf16[2,256,1024]{2,1,0:T(8,128)(2,1)}, bf16[2,256,1024]{2,1,0:T(8,128)(2,1)}, u32[]{:S(2)}, u32[]{:S(2)}) collective-permute-start(bf16[2,256,1024]{2,1,0:T(8,128)(2,1)} %get-tuple-element.35), channel_id=1, source_target_pairs={{0,16},{8,24},{16,0},{24,8},{1,17},{9,25},{17,1},{25,9},{2,18},{10... | collective-permute-start | bytes 3145736 | tf_op jit(solution)/shard_map/ppermute | solution.py:23
  401.9 19.2 %copy-start.4 = (bf16[1,2,256,1024]{3,2,1,0:T(8,128)(2,1)S(1)}, bf16[1,2,256,1024]{3,2,1,0:T(8,128)(2,1)}, u32[]{:S(2)}) copy-start(bf16[1,2,256,1024]{3,2,1,0:T(8,128)(2,1)} %get-tuple-element.34) | copy-start | bytes 3145732
  401.9 103.3 %reduce-scatter.22.cloned.1.call-start = ((), (), s32[]{:S(2)}) async-start(), calls=%async_computation.19 | async-start | bytes 1769472 | tf_op jit(solution)/shard_map/reduce_scatter | solution.py:122
  424.5 8.7 %copy-start.18 = (bf16[1024,768]{0,1:T(8,128)(2,1)S(1)}, bf16[1024,768]{0,1:T(8,128)(2,1)}, u32[]{:S(2)}) copy-start(bf16[1024,768]{0,1:T(8,128)(2,1)} %convolution_convert_fusion.7) | copy-start | bytes 4718596
  465.3 74.2 %reduce-scatter.26.cloned.1.call-start = ((), (), s32[]{:S(2)}) async-start(), calls=%async_computation.21 | async-start | bytes 2359296 | tf_op jit(solution)/shard_map/reduce_scatter | solution.py:128
  472.8 99.1 %reduce-scatter.24.cloned.1.call-start = ((), (), s32[]{:S(2)}) async-start(), calls=%async_computation.20 | async-start | bytes 589824 | tf_op jit(solution)/shard_map/reduce_scatter | solution.py:128
  477.0 131.2 %reduce-scatter.20.cloned.1.call-start = ((), (), s32[]{:S(2)}) async-start(), calls=%async_computation.18 | async-start | bytes 2621440 | tf_op jit(solution)/shard_map/reduce_scatter | solution.py:136
  485.7 19.5 %all-to-all-start.3 = ((bf16[4,32,1024]{2,1,0:T(8,128)(2,1)}), bf16[4,32,1024]{2,1,0:T(8,128)(2,1)S(1)}, u32[]{:S(2)}, u32[]{:S(2)}) async-start(bf16[4,32,1024]{2,1,0:T(8,128)(2,1)} %dynamic-slice_bitcast_fusion), calls=%async_computation.9 | async-start | bytes 524288 | tf_op jit(solution)/shard_map/all_to_all | solution.py:123
  505.2 68.2 %all-to-all-start.2 = ((bf16[4,32,768]{2,1,0:T(8,128)(2,1)}), bf16[4,32,768]{2,1,0:T(8,128)(2,1)S(1)}, u32[]{:S(2)}, u32[]{:S(2)}) async-start(bf16[4,32,768]{2,1,0:T(8,128)(2,1)} %bitcast.344), calls=%async_computation.7 | async-start | bytes 393216 | tf_op jit(solution)/shard_map/all_to_all | solution.py:123
  509.0 236.0 %reduce-scatter.28.cloned.1.call-start = ((), (), s32[]{:S(2)}) async-start(), calls=%async_computation.22 | async-start | bytes 540672
  509.4 98.8 %copy-start.23 = (f32[1,1024]{1,0:T(1,128)S(1)}, f32[1,1024]{1,0:T(1,128)}, u32[]{:S(2)}) copy-start(f32[1,1024]{1,0:T(1,128)} %copy-done.22) | copy-start | bytes 12292
  509.4 98.8 %copy-start.26 = (f32[256]{0:T(256)S(1)}, f32[256]{0:T(256)}, u32[]{:S(2)}) copy-start(f32[256]{0:T(256)} %copy-done.25) | copy-start | bytes 3076
  509.4 98.8 %copy-start.28 = (f32[256]{0:T(256)S(1)}, f32[256]{0:T(256)}, u32[]{:S(2)}) copy-start(f32[256]{0:T(256)} %copy-done.27) | copy-start | bytes 3076
  (19 other events, 39.1 us)
Sparse Core Ops, SparseCore 0:
  59.7 21.4 all-gather.6
  147.4 32.6 reduce-scatter.13
  182.4 29.1 all-gather.8
  213.0 28.5 all-gather.10
  248.9 34.7 reduce-scatter.15
  340.4 35.1 reduce-scatter.17
  402.0 64.8 all-reduce.3
  469.3 33.6 reduce-scatter.21
  505.4 34.0 reduce-scatter.25
  542.3 29.5 reduce-scatter.23
  574.9 33.3 reduce-scatter.19
  611.2 133.8 reduce-scatter.27
